TPU v7x, 32 devices: a whole 2x2x4 slice. The times are simulated.
32 devices in a mesh: expert: 16 (over z, y, x), dp: 2 (over core).
Axes of the slice: x: 2, y: 2, z: 4, core: 2. Of those that a mesh axis runs over, the one named last changes fastest.
Arguments:
- tokens: bfloat16 [2048, 2048], P(('expert', 'dp')), may hold values from -6 to 6
- expert_ids: int32 [2048, 8], P(('expert', 'dp')), may hold values from 0 to 15, all different within a row; in each aligned block of 64 rows (0 to 63, 64 to 127, ...) at most 48 rows name the same one
- gate_probs: float32 [2048, 8], P(('expert', 'dp')), may hold values from 0.05 to 1
- swap_flags: int32 [8], replicated, may hold values from 0 to 1, as said below
- w_gate: bfloat16 [16, 2048, 768], P('expert', 'dp'), may hold values from -0.125 to 0.125
- w_up: bfloat16 [16, 2048, 768], P('expert', 'dp'), may hold values from -0.125 to 0.125
- w_down: bfloat16 [16, 768, 2048], P('expert', None, 'dp'), may hold values from -0.21875 to 0.21875
Outputs:
- moe_out: bfloat16 [2048, 2048], P(('expert', 'dp'))
Inputs may be any that keep to these rules, and one draw needn't show every extreme that they name: `expert_ids`: each row names 8 different experts. Within the 64 rows of one device no expert is named by more than 48 rows, a bound that some block reaches. swap_flags[0] is 1; the other entries are 0 or 1.
All inputs are finite; a program needn't handle non-finite values.
Results may differ from a plain program's by a relative error of at most 0.0057.
Values may be sent and summed in bfloat16 or wider, within the bound.
A program may use at most 64 MiB of HBM per device.

v0:
```python
import jax
import jax.numpy as jnp
from jax import lax
from jax.sharding import PartitionSpec as P


def on_device(tokens, expert_ids, gate_probs, swap_flags, w_gate, w_up, w_down):
    axis_size = lax.axis_size("expert")
    own_index = lax.axis_index("expert")
    half_span = axis_size // 2
    shares = gate_probs / jnp.sum(gate_probs, axis=1, keepdims=True)
    experts = jnp.arange(axis_size, dtype=jnp.int32)
    dense = jnp.sum(
        jnp.where(expert_ids[:, :, None] == experts[None, None, :], shares[:, :, None], 0.0), axis=1
    )
    lower = own_index < half_span
    own_base = jnp.where(lower, own_index, own_index - half_span)
    own_flag = (
        jnp.sum(jnp.where(jnp.arange(half_span, dtype=jnp.int32) == own_base, swap_flags, 0)) == 1
    )
    served = jnp.where(
        own_flag, jnp.where(lower, own_index + half_span, own_index - half_span), own_index
    )
    rows = lax.all_gather(tokens, "expert", axis=0, tiled=True)
    dense_all = lax.all_gather(dense, "expert", axis=0, tiled=True)
    factor = jnp.sum(jnp.where(experts[None, :] == served, dense_all, 0.0), axis=1)
    gate_next = jnp.dot(
        rows,
        lax.all_gather(w_gate, "dp", axis=1, tiled=True)[0],
        preferred_element_type=jnp.float32,
    )
    up_next = jnp.dot(
        rows, lax.all_gather(w_up, "dp", axis=1, tiled=True)[0], preferred_element_type=jnp.float32
    )
    hidden = (jax.nn.silu(gate_next) * up_next).astype(jnp.bfloat16)
    produced = jnp.dot(
        hidden,
        lax.all_gather(w_down, "dp", axis=2, tiled=True)[0],
        preferred_element_type=jnp.float32,
    ).astype(jnp.bfloat16)
    partial = (factor[:, None] * produced.astype(jnp.float32)).astype(jnp.bfloat16)
    return lax.psum_scatter(partial, "expert", scatter_dimension=0, tiled=True)


def solution(mesh):
    placed = (
        P(("expert", "dp"), None),
        P(("expert", "dp"), None),
        P(("expert", "dp"), None),
        P(),
        P("expert", "dp", None),
        P("expert", "dp", None),
        P("expert", None, "dp"),
    )
    return jax.shard_map(
        on_device, mesh=mesh, in_specs=placed, out_specs=P(("expert", "dp"), None), check_vma=False
    )
```

profile of v0, /device:TPU:0, one launch (start us, length us, event | category | flops | bytes accessed | tf_op | source)
XLA Modules:
  0.0 246.6 jit_solution(10669585378727031929)
XLA Ops:
  6.5 0.0 all-gather.10.cloned.1.call-start
  6.5 0.7 all-gather.10.cloned.1.call-update
  7.3 0.0 all-gather.6.cloned.1.call-start
  7.3 0.7 all-gather.6.cloned.1.call-update
  8.0 0.0 all-gather.8.cloned.1.call-start
  8.1 0.7 all-gather.8.cloned.1.call-update
  8.7 0.0 all-gather.12.cloned.1.call-start
  8.8 0.5 all-gather.12.cloned.1.call-update
  9.3 0.0 reduce-scatter.2.cloned.1.call-start
  9.4 0.0 copy-done
  9.4 0.0 copy-done.1
  9.5 43.1 %all-gather = f32[16,64,16]{1,2,0:T(8,128)S(1)} all-gather(f32[1,64,16]{1,2,0:T(8,128)S(1)} %bitcast.18), channel_id=1, replica_groups=mesh['expert'=16,'dp'=2] {'expert'}, dimensions={0}, use_global_device_ids=true | all-gather | bytes 69632 | tf_op jit(solution)/shard_map/all_gather | solution.py:25
  52.6 0.1 reshape.10
  52.7 0.0 copy-done.2
  52.7 0.6 fusion.9
  54.0 0.1 select_reduce_fusion
  54.1 0.0 all-gather.10.cloned.1.call-done
  54.1 49.5 %all-gather.6.cloned.1.call-done = bf16[1024,2048]{1,0:T(8,128)(2,1)} async-done(((bf16[64,2048]{1,0:T(8,128)(2,1)}), bf16[1024,2048]{1,0:T(8,128)(2,1)}) %all-gather.6.cloned.1.call-update) | async-done | bytes 4194320 | tf_op jit(solution)/shard_map/all_gather | solution.py:24
  103.7 6.1 %fusion.1 = f32[1024,768]{1,0:T(8,128)S(1)} fusion(bf16[1024,2048]{1,0:T(8,128)(2,1)} %all-gather.6.cloned.1.call-done, bf16[1,2048,768]{2,1,0:T(8,128)(2,1)} %all-gather.10.cloned.1.call-done), kind=kOutput, calls=%fused_computation.2 | convolution fusion | flops 3221225472 | bytes 10485760 | tf_op jit(solution)/shard_map/dot_general | solution.py:32
  109.8 6.2 %all-gather.8.cloned.1.call-done = bf16[1,2048,768]{2,1,0:T(8,128)(2,1)} async-done(((bf16[1,1024,768]{2,1,0:T(8,128)(2,1)}), bf16[1,2048,768]{2,1,0:T(8,128)(2,1)}) %all-gather.8.cloned.1.call-update) | async-done | bytes 3145744 | tf_op jit(solution)/shard_map/all_gather | solution.py:29
  116.0 14.7 %all-gather.12.cloned.1.call-done = bf16[1,768,2048]{2,1,0:T(8,128)(2,1)} async-done(((bf16[1,768,1024]{2,1,0:T(8,128)(2,1)}), bf16[1,768,2048]{2,1,0:T(8,128)(2,1)}) %all-gather.12.cloned.1.call-update) | async-done | bytes 3145744 | tf_op jit(solution)/shard_map/all_gather | solution.py:38
  130.7 12.8 %multiply_convert_fusion = bf16[1024,2048]{1,0:T(8,128)(2,1)} fusion(f32[1024]{0:T(1024)S(1)} %select_reduce_fusion, bf16[1,768,2048]{2,1,0:T(8,128)(2,1)} %all-gather.12.cloned.1.call-done, f32[1024,768]{1,0:T(8,128)S(1)} %fusion.1, bf16[1024,2048]{1,0:T(8,128)(2,1)} %all-gather.6.cloned.1.call-done, bf16[1,2048,768]{2,1,0:T(8,128)(2,1)} %all-gather.8.cloned.1.call-done), kind=kOutput, calls=%fused_computation | convolution fusion | flops 6455558144 | bytes 17829888 | tf_op jit(solution)/shard_map/dot_general | solution.py:36
  143.5 0.0 reduce-scatter.2.cloned.1.call-update
  143.6 96.5 %reduce-scatter.2.cloned.1.call-done = bf16[64,2048]{1,0:T(8,128)(2,1)} async-done(((bf16[1024,2048]{1,0:T(8,128)(2,1)}), bf16[64,2048]{1,0:T(8,128)(2,1)}) %reduce-scatter.2.cloned.1.call-update) | async-done | bytes 262160 | tf_op jit(solution)/shard_map/reduce_scatter | solution.py:42
  (8 shorter events, 0.1 us)
Async XLA Ops:
  6.5 2.8 %copy-start = (f32[64,8]{0,1:T(8,128)S(1)}, f32[64,8]{0,1:T(8,128)}, u32[]{:S(2)}) copy-start(f32[64,8]{0,1:T(8,128)} %param.9) | copy-start | bytes 6148
  6.5 2.9 %copy-start.1 = (s32[64,8]{0,1:T(8,128)S(1)}, s32[64,8]{0,1:T(8,128)}, u32[]{:S(2)}) copy-start(s32[64,8]{0,1:T(8,128)} %param.8) | copy-start | bytes 6148
  6.5 46.2 %copy-start.2 = (s32[8]{0:T(128)S(1)}, s32[8]{0:T(128)}, u32[]{:S(2)}) copy-start(s32[8]{0:T(128)} %param.10) | copy-start | bytes 100
  6.5 47.6 %all-gather.10.cloned.1.call-start = ((), (), s32[]{:S(2)}) async-start(), calls=%async_computation.3 | async-start | bytes 4718592 | tf_op jit(solution)/shard_map/all_gather | solution.py:33
  7.3 96.4 %all-gather.6.cloned.1.call-start = ((), (), s32[]{:S(2)}) async-start(), calls=%async_computation.1 | async-start | bytes 4456448 | tf_op jit(solution)/shard_map/all_gather | solution.py:24
  8.0 108.0 %all-gather.8.cloned.1.call-start = ((), (), s32[]{:S(2)}) async-start(), calls=%async_computation.2 | async-start | bytes 4718592 | tf_op jit(solution)/shard_map/all_gather | solution.py:29
  8.7 121.9 %all-gather.12.cloned.1.call-start = ((), (), s32[]{:S(2)}) async-start(), calls=%async_computation.4 | async-start | bytes 4718592 | tf_op jit(solution)/shard_map/all_gather | solution.py:38
  9.3 230.7 %reduce-scatter.2.cloned.1.call-start = ((), (), s32[]{:S(2)}) async-start(), calls=%async_computation.5 | async-start | bytes 4456448 | tf_op jit(solution)/shard_map/reduce_scatter | solution.py:42
Sparse Core Ops, SparseCore 0:
  8.9 14.8 all-gather.9
  26.5 77.0 all-gather.5
  105.2 10.7 all-gather.7
  117.4 13.2 all-gather.11
  143.7 96.3 reduce-scatter.1
where the time goes:
time: 247 us
  waiting for transfers between devices  170 us (69%)
  blocking collectives  43.1 us (17%)
  matrix products  19 us (8%)
  between operations  13.9 us (6%)
    reduce_scatter x1, waiting for transfers between devices, on_device(): return lax.psum_scatter(partial, 'expert', scatter_dimension=0, tiled=True)  96.5 us
    all_gather x1, waiting for transfers between devices, on_device(): rows = lax.all_gather(tokens, 'expert', axis=0, tiled=True)  49.5 us
    all_gather x1, blocking collectives, on_device(): dense_all = lax.all_gather(dense, 'expert', axis=0, tiled=True)  43.1 us
    all_gather x1, waiting for transfers between devices, on_device(): lax.all_gather(w_down, 'dp', axis=2, tiled=True)[0]  14.7 us
    dot_general x1, matrix products, on_device(): jnp.dot(hidden, lax.all_gather(w_down, 'dp', axis=2, tiled=True)[0], pref...  12.8 us
    all_gather x1, waiting for transfers between devices, on_device(): lax.all_gather(w_gate, 'dp', axis=1, tiled=True)[0]  6.18 us
    dot_general x1, matrix products, on_device(): jnp.dot(rows, lax.all_gather(w_up, 'dp', axis=1, tiled=True)[0], preferre...  6.12 us
  transfers between devices with their start and end apart: 5, of which 4 were waited for; matrix products, arithmetic and copies ran while one was open for 3% of the time, Pallas kernels for 0%

commit v1 on v0

--- a/solution.py
+++ b/solution.py
@@ -2,6 +2,23 @@
 import jax.numpy as jnp
 from jax import lax
 from jax.sharding import PartitionSpec as P
+
+
+def laid_out(parts, dim):
+    parts = jnp.moveaxis(parts, 0, dim)
+    dims = parts.shape
+    return parts.reshape(*dims[:dim], dims[dim] * dims[dim + 1], *dims[dim + 2 :])
+
+
+def doubled(shard, axis):
+    devices, position = (lax.axis_size(axis), lax.axis_index(axis))
+    parts, apart = (shard[None], 1)
+    while apart < devices:
+        received = lax.ppermute(parts, axis, [(i, i ^ apart) for i in range(devices)])
+        low = position & apart == 0
+        parts = jnp.concatenate([jnp.where(low, parts, received), jnp.where(low, received, parts)])
+        apart *= 2
+    return parts
 
 
 def on_device(tokens, expert_ids, gate_probs, swap_flags, w_gate, w_up, w_down):
@@ -22,7 +39,7 @@
         own_flag, jnp.where(lower, own_index + half_span, own_index - half_span), own_index
     )
     rows = lax.all_gather(tokens, "expert", axis=0, tiled=True)
-    dense_all = lax.all_gather(dense, "expert", axis=0, tiled=True)
+    dense_all = laid_out(doubled(dense, "expert"), 0)
     factor = jnp.sum(jnp.where(experts[None, :] == served, dense_all, 0.0), axis=1)
     gate_next = jnp.dot(
         rows,

time: 247 us -> 247 us (level)
  blocking collectives: 43.1 us -> 0 us
  waiting for transfers between devices: 170 us -> 202 us
  starting transfers between devices: 0.15 us -> 10.5 us
    all_gather x1 -> x0, blocking collectives: 43.1 us -> none  [on_device(): dense_all = lax.all_gather(dense, 'expert', axis=0, tiled=True)]
    all_gather x1, waiting for transfers between devices: 49.5 us -> 76.3 us  [on_device(): rows = lax.all_gather(tokens, 'expert', axis=0, tiled=True)]
    ppermute x0 -> x4, starting transfers between devices: none -> 10.4 us  [doubled(): lax.ppermute(parts, axis, [(i, i ^ apart) for i in range(devices)])]
    ppermute x0 -> x4, waiting for transfers between devices: none -> 6.16 us  [doubled(): lax.ppermute(parts, axis, [(i, i ^ apart) for i in range(devices)])]
  transfers between devices with their start and end apart: 5 -> 9, of which waited for: 4 -> 8; matrix products, arithmetic and copies ran while one was open for 3% -> 3% of each run, Pallas kernels for 0% -> 0%
where the time goes in v1:
time: 247 us
  waiting for transfers between devices  202 us (82%)
  matrix products  19 us (8%)
  between operations  13.9 us (6%)
  starting transfers between devices  10.5 us (4%)
    reduce_scatter x1, waiting for transfers between devices, on_device(): return lax.psum_scatter(partial, 'expert', scatter_dimension=0, tiled=True)  96.5 us
    all_gather x1, waiting for transfers between devices, on_device(): rows = lax.all_gather(tokens, 'expert', axis=0, tiled=True)  76.3 us
    all_gather x1, waiting for transfers between devices, on_device(): lax.all_gather(w_down, 'dp', axis=2, tiled=True)[0]  14.7 us
    dot_general x1, matrix products, on_device(): jnp.dot(hidden, lax.all_gather(w_down, 'dp', axis=2, tiled=True)[0], pref...  12.8 us
    ppermute x4, starting transfers between devices, doubled(): lax.ppermute(parts, axis, [(i, i ^ apart) for i in range(devices)])  10.4 us
    all_gather x1, waiting for transfers between devices, on_device(): lax.all_gather(w_gate, 'dp', axis=1, tiled=True)[0]  6.18 us
    ppermute x4, waiting for transfers between devices, doubled(): lax.ppermute(parts, axis, [(i, i ^ apart) for i in range(devices)])  6.16 us
    dot_general x1, matrix products, on_device(): jnp.dot(rows, lax.all_gather(w_up, 'dp', axis=1, tiled=True)[0], preferre...  6.12 us
  transfers between devices with their start and end apart: 9, of which 8 were waited for; matrix products, arithmetic and copies ran while one was open for 3% of the time, Pallas kernels for 0%

profile of v1, /device:TPU:0, one launch (start us, length us, event | category | flops | bytes accessed | tf_op | source)
XLA Modules:
  0.0 246.7 jit_solution(11176733526094126552)
XLA Ops:
  6.5 0.7 all-gather.9.cloned.1.call-update
  7.3 0.0 all-gather.5.cloned.1.call-start
  7.3 0.7 all-gather.5.cloned.1.call-update
  8.0 0.0 all-gather.7.cloned.1.call-start
  8.1 0.7 all-gather.7.cloned.1.call-update
  8.8 0.5 all-gather.11.cloned.1.call-update
  9.3 0.0 reduce-scatter.2.cloned.1.call-start
  9.4 3.0 %collective-permute-start = (f32[1,64,16]{1,2,0:T(8,128)S(1)}, f32[1,64,16]{1,2,0:T(8,128)S(1)}, u32[]{:S(2)}, u32[]{:S(2)}) collective-permute-start(f32[1,64,16]{1,2,0:T(8,128)S(1)} %bitcast.18), channel_id=1, source_target_pairs={{0,2},{2,0},{4,6},{6,4},{8,10},{10,8},{12,14},{14,12},{16,18},{18,... | collective-permute-start | bytes 12296 | tf_op jit(solution)/shard_map/ppermute | solution.py:17
  12.5 1.6 collective-permute-done
  14.1 2.1 collective-permute-start.1
  16.2 1.7 collective-permute-done.1
  17.9 2.1 collective-permute-start.2
  20.1 0.6 fusion.10
  21.4 0.6 collective-permute-done.2
  22.0 3.1 %collective-permute-start.3 = (f32[8,64,16]{1,2,0:T(8,128)S(1)}, f32[8,64,16]{1,2,0:T(8,128)S(1)}, u32[]{:S(2)}, u32[]{:S(2)}) collective-permute-start(f32[8,64,16]{1,2,0:T(8,128)S(1)} %pad_maximum_fusion), channel_id=1, source_target_pairs={{0,16},{2,18},{4,20},{6,22},{8,24},{10,26},{12,28},{14,30},{16,0},... | collective-permute-start | bytes 98312 | tf_op jit(solution)/shard_map/ppermute | solution.py:17
  25.1 2.2 collective-permute-done.3
  27.4 0.1 fusion.9
  27.5 0.1 mul.17
  27.6 76.3 %all-gather.5.cloned.1.call-done = bf16[1024,2048]{1,0:T(8,128)(2,1)} async-done(((bf16[64,2048]{1,0:T(8,128)(2,1)}), bf16[1024,2048]{1,0:T(8,128)(2,1)}) %all-gather.5.cloned.1.call-update) | async-done | bytes 4194320 | tf_op jit(solution)/shard_map/all_gather | solution.py:41
  103.8 6.1 %fusion.1 = f32[1024,768]{1,0:T(8,128)S(1)} fusion(bf16[1024,2048]{1,0:T(8,128)(2,1)} %all-gather.5.cloned.1.call-done, bf16[1,2048,768]{2,1,0:T(8,128)(2,1)} %all-gather.9.cloned.1.call-done), kind=kOutput, calls=%fused_computation.2 | convolution fusion | flops 3221225472 | bytes 10485760 | tf_op jit(solution)/shard_map/dot_general | solution.py:49
  110.0 6.2 %all-gather.7.cloned.1.call-done = bf16[1,2048,768]{2,1,0:T(8,128)(2,1)} async-done(((bf16[1,1024,768]{2,1,0:T(8,128)(2,1)}), bf16[1,2048,768]{2,1,0:T(8,128)(2,1)}) %all-gather.7.cloned.1.call-update) | async-done | bytes 3145744 | tf_op jit(solution)/shard_map/all_gather | solution.py:46
  116.1 14.7 %all-gather.11.cloned.1.call-done = bf16[1,768,2048]{2,1,0:T(8,128)(2,1)} async-done(((bf16[1,768,1024]{2,1,0:T(8,128)(2,1)}), bf16[1,768,2048]{2,1,0:T(8,128)(2,1)}) %all-gather.11.cloned.1.call-update) | async-done | bytes 3145744 | tf_op jit(solution)/shard_map/all_gather | solution.py:55
  130.9 12.8 %multiply_convert_fusion = bf16[1024,2048]{1,0:T(8,128)(2,1)} fusion(f32[1024]{0:T(1024)S(1)} %mul.17, bf16[1,768,2048]{2,1,0:T(8,128)(2,1)} %all-gather.11.cloned.1.call-done, f32[1024,768]{1,0:T(8,128)S(1)} %fusion.1, bf16[1024,2048]{1,0:T(8,128)(2,1)} %all-gather.5.cloned.1.call-done, bf16[1,2048,768]{2,1,0:T(8,128)(2,1)} %all-gather.7.cloned.1.call-done), kind=kOutput, calls=%fused_computation | convolution fusion | flops 6455558144 | bytes 17829888 | tf_op jit(solution)/shard_map/dot_general | solution.py:53
  143.7 96.5 %reduce-scatter.2.cloned.1.call-done = bf16[64,2048]{1,0:T(8,128)(2,1)} async-done(((bf16[1024,2048]{1,0:T(8,128)(2,1)}), bf16[64,2048]{1,0:T(8,128)(2,1)}) %reduce-scatter.2.cloned.1.call-update) | async-done | bytes 262160 | tf_op jit(solution)/shard_map/reduce_scatter | solution.py:59
  (21 shorter events, 0.2 us)
Async XLA Ops:
  6.5 2.8 %copy-start = (f32[64,8]{0,1:T(8,128)S(1)}, f32[64,8]{0,1:T(8,128)}, u32[]{:S(2)}) copy-start(f32[64,8]{0,1:T(8,128)} %param.9) | copy-start | bytes 6148
  6.5 2.9 %copy-start.1 = (s32[64,8]{0,1:T(8,128)S(1)}, s32[64,8]{0,1:T(8,128)}, u32[]{:S(2)}) copy-start(s32[64,8]{0,1:T(8,128)} %param.8) | copy-start | bytes 6148
  6.5 13.5 %copy-start.2 = (s32[8]{0:T(128)S(1)}, s32[8]{0:T(128)}, u32[]{:S(2)}) copy-start(s32[8]{0:T(128)} %param.10) | copy-start | bytes 100
  6.5 21.0 %all-gather.9.cloned.1.call-start = ((), (), s32[]{:S(2)}) async-start(), calls=%async_computation.3 | async-start | bytes 4718592 | tf_op jit(solution)/shard_map/all_gather | solution.py:50
  7.3 96.6 %all-gather.5.cloned.1.call-start = ((), (), s32[]{:S(2)}) async-start(), calls=%async_computation.1 | async-start | bytes 4456448 | tf_op jit(solution)/shard_map/all_gather | solution.py:41
  8.0 108.1 %all-gather.7.cloned.1.call-start = ((), (), s32[]{:S(2)}) async-start(), calls=%async_computation.2 | async-start | bytes 4718592 | tf_op jit(solution)/shard_map/all_gather | solution.py:46
  8.7 122.1 %all-gather.11.cloned.1.call-start = ((), (), s32[]{:S(2)}) async-start(), calls=%async_computation.4 | async-start | bytes 4718592 | tf_op jit(solution)/shard_map/all_gather | solution.py:55
  9.3 230.9 %reduce-scatter.2.cloned.1.call-start = ((), (), s32[]{:S(2)}) async-start(), calls=%async_computation.5 | async-start | bytes 4456448 | tf_op jit(solution)/shard_map/reduce_scatter | solution.py:59
  9.4 4.6 %collective-permute-start = (f32[1,64,16]{1,2,0:T(8,128)S(1)}, f32[1,64,16]{1,2,0:T(8,128)S(1)}, u32[]{:S(2)}, u32[]{:S(2)}) collective-permute-start(f32[1,64,16]{1,2,0:T(8,128)S(1)} %bitcast.18), channel_id=1, source_target_pairs={{0,2},{2,0},{4,6},{6,4},{8,10},{10,8},{12,14},{14,12},{16,18},{18,... | collective-permute-start | bytes 12296 | tf_op jit(solution)/shard_map/ppermute | solution.py:17
  14.1 3.8 %collective-permute-start.1 = (f32[2,64,16]{1,2,0:T(8,128)S(1)}, f32[2,64,16]{1,2,0:T(8,128)S(1)}, u32[]{:S(2)}, u32[]{:S(2)}) collective-permute-start(f32[2,64,16]{1,2,0:T(8,128)S(1)} %pad_maximum_fusion.2), channel_id=1, source_target_pairs={{0,4},{2,6},{4,0},{6,2},{8,12},{10,14},{12,8},{14,10},{16,20},{18,... | collective-permute-start | bytes 24584 | tf_op jit(solution)/shard_map/ppermute | solution.py:17
  17.9 4.0 %collective-permute-start.2 = (f32[4,64,16]{1,2,0:T(8,128)S(1)}, f32[4,64,16]{1,2,0:T(8,128)S(1)}, u32[]{:S(2)}, u32[]{:S(2)}) collective-permute-start(f32[4,64,16]{1,2,0:T(8,128)S(1)} %pad_maximum_fusion.1), channel_id=1, source_target_pairs={{0,8},{2,10},{4,12},{6,14},{8,0},{10,2},{12,4},{14,6},{16,24},{18,... | collective-permute-start | bytes 49160 | tf_op jit(solution)/shard_map/ppermute | solution.py:17
  22.0 5.4 %collective-permute-start.3 = (f32[8,64,16]{1,2,0:T(8,128)S(1)}, f32[8,64,16]{1,2,0:T(8,128)S(1)}, u32[]{:S(2)}, u32[]{:S(2)}) collective-permute-start(f32[8,64,16]{1,2,0:T(8,128)S(1)} %pad_maximum_fusion), channel_id=1, source_target_pairs={{0,16},{2,18},{4,20},{6,22},{8,24},{10,26},{12,28},{14,30},{16,0},... | collective-permute-start | bytes 98312 | tf_op jit(solution)/shard_map/ppermute | solution.py:17
Sparse Core Ops, SparseCore 0:
  8.9 14.8 all-gather.8
  26.5 77.2 all-gather.4
  105.4 10.7 all-gather.6
  117.5 13.2 all-gather.10
  143.8 96.3 reduce-scatter.1
